TPU v7x, 256 devices: a whole 4x4x8 slice. The times are simulated.
256 devices in a mesh: contact: 32 (over y, x, core), body: 8 (over z).
Axes of the slice: x: 4, y: 4, z: 8, core: 2. Of those that a mesh axis runs over, the one named last changes fastest.
Arguments:
- jacobian: bfloat16 [4096, 2, 384, 384], P(('contact', 'body')), may hold values from -0.21875 to 0.21875
- tile_block: int32 [4096, 2], P(('contact', 'body')), may hold values from 0 to 31
- tile_count: int32 [256], P(('contact', 'body')), may hold values from 8 to 16, as said below
- vel_free: float32 [256, 384], P('body'), may hold values from -6 to 6
- inv_mass: float32 [256, 384], P('body'), may hold values from 0.25 to 2
- bias: float32 [4096, 384], P(('contact', 'body')), may hold values from -6 to 6
- step_scale: float32 [4096, 384], P(('contact', 'body')), may hold values from 0.05 to 0.5
- friction: float32 [4096, 128], P(('contact', 'body')), may hold values from 0.2 to 1
- impulse_start: float32 [4096, 384], P(('contact', 'body')), may hold values from -6 to 6
Outputs:
- impulse: float32 [4096, 384], P(('contact', 'body'))
- velocity: float32 [256, 384], P('body')
Inputs may be any that keep to these rules, and one draw needn't show every extreme that they name: `tile_count`: some device has all 16 tile slots live in every draw.
All inputs are finite; a program needn't handle non-finite values.
Results may differ from a plain program's by a relative error of at most 0.0062.
Values may be sent and summed in bfloat16 or wider, within the bound.
A program may use at most 64 MiB of HBM per device.

v0:
```python
import jax
import jax.numpy as jnp
from jax import lax
from jax.sharding import PartitionSpec as P

ITERS = 2


def shifted(value, axis, steps):
    count = lax.axis_size(axis)
    pairs = [(source, (source + steps) % count) for source in range(count)]
    return lax.ppermute(value, axis, pairs)


def project(trial, friction, contacts):
    normal = trial[:, :contacts]
    first = trial[:, contacts : 2 * contacts]
    second = trial[:, 2 * contacts :]
    tangent = jnp.sqrt(first * first + second * second)
    inside = tangent <= friction * normal
    below = friction * tangent <= -normal
    moved = (normal + friction * tangent) / (1.0 + friction * friction)
    safe = jnp.where(inside | below, 1.0, tangent)
    factor = jnp.where(inside, 1.0, jnp.where(below, 0.0, friction * moved / safe))
    new_normal = jnp.where(inside, normal, jnp.where(below, 0.0, moved))
    return jnp.concatenate([new_normal, first * factor, second * factor], axis=1)


def per_device(
    jacobian, tile_block, tile_count, vel_free, inv_mass, bias, step_scale, friction, impulse_start
):
    tiles_here = jacobian.shape[0]
    slab_blocks = vel_free.shape[0]
    contacts = friction.shape[1]
    order = jnp.arange(tiles_here, dtype=jnp.int32)
    mask = (order < tile_count[0]).astype(jnp.float32)[:, None]
    span = jnp.arange(slab_blocks, dtype=jnp.int32)
    pick_own = (tile_block[:, 0:1] == span[None, :]).astype(jnp.float32)
    pick_next = (tile_block[:, 1:2] == span[None, :]).astype(jnp.float32)
    pick_own_b = pick_own.astype(jnp.bfloat16)
    pick_next_b = pick_next.astype(jnp.bfloat16)

    def merged_partials(lam):
        lamb = lam.astype(jnp.bfloat16)
        push = jnp.einsum("tkbc,tc->tkb", jacobian, lamb, preferred_element_type=jnp.float32)
        own = jnp.einsum("ts,tb->sb", pick_own, push[:, 0], precision=lax.Precision.HIGHEST)
        later = jnp.einsum("ts,tb->sb", pick_next, push[:, 1], precision=lax.Precision.HIGHEST)
        return own + shifted(later, "body", 1)

    def slab_total(lam):
        return lax.psum(merged_partials(lam), "contact")

    lam = impulse_start * mask
    for sweep in range(ITERS):
        total = slab_total(lam)
        velb = (vel_free + inv_mass * total).astype(jnp.bfloat16)
        velb_next = shifted(velb, "body", -1)
        rows_own = jnp.dot(pick_own_b, velb, preferred_element_type=jnp.float32).astype(
            jnp.bfloat16
        )
        rows_next = jnp.dot(pick_next_b, velb_next, preferred_element_type=jnp.float32).astype(
            jnp.bfloat16
        )
        rows = jnp.stack([rows_own, rows_next], axis=1)
        rel = jnp.einsum("tkbc,tkb->tc", jacobian, rows, preferred_element_type=jnp.float32) + bias
        lam = project(lam - step_scale * rel, friction, contacts) * mask
    total = slab_total(lam)
    velocity = vel_free + inv_mass * total
    return (lam, velocity)


def solution(mesh):
    placed = (
        P(("contact", "body"), None, None, None),
        P(("contact", "body"), None),
        P(("contact", "body")),
        P("body", None),
        P("body", None),
        P(("contact", "body"), None),
        P(("contact", "body"), None),
        P(("contact", "body"), None),
        P(("contact", "body"), None),
    )
    return jax.shard_map(
        per_device,
        mesh=mesh,
        in_specs=placed,
        out_specs=(P(("contact", "body"), None), P("body", None)),
        check_vma=False,
    )
```

profile of v0, /device:TPU:0, one launch (start us, length us, event | category | flops | bytes accessed | tf_op | source)
XLA Modules:
  0.0 435.7 jit_solution(17397203647870327549)
XLA Ops:
  0.6 0.0 copy-start.1
  0.6 0.0 copy-start
  1.3 0.8 slice_bitcast_fusion.1
  2.1 0.8 fusion.35
  2.9 0.0 copy-start.2
  2.9 0.0 copy-start.3
  2.9 0.0 copy-start.4
  2.9 0.0 copy-start.5
  2.9 6.2 %fusion.31 = f32[16,1,2,384]{3,1,2,0:T(1,128)S(1)} fusion(bf16[16,2,384,384]{3,2,1,0:T(8,128)(2,1)} %param.9, bf16[16,384,1,1]{1,0,2,3:T(8,128)(2,1)S(1)} %fusion.35), kind=kOutput, calls=%fused_computation.50 | convolution fusion | flops 9437184 | bytes 9498624 | tf_op jit(solution)/shard_map/tkbc,tc->tkb/dot_general | solution.py:45
  9.3 0.3 fusion.18
  9.6 0.3 collective-permute-start
  9.8 6.0 %collective-permute-done = f32[32,384]{1,0:T(8,128)S(1)} collective-permute-done((f32[32,384]{1,0:T(8,128)S(1)}, f32[32,384]{1,0:T(8,128)S(1)}, u32[]{:S(2)}, u32[]{:S(2)}) %collective-permute-start) | collective-permute-done | bytes 49184 | tf_op jit(solution)/shard_map/ppermute | solution.py:12
  15.8 0.3 convolution_add_fusion.2
  16.1 127.5 %psum.21 = f32[32,384]{1,0:T(8,128)S(1)} all-reduce(f32[32,384]{1,0:T(8,128)S(1)} %convolution_add_fusion.2), channel_id=1, replica_groups=mesh['contact'=32,'body'=8] {'contact'}, use_global_device_ids=true, to_apply=%region_0.0 | all-reduce | flops 12288 | bytes 98304 | tf_op jit(solution)/shard_map/psum | solution.py:51
  143.6 0.0 copy-done.1
  143.6 0.0 copy-done
  143.7 1.8 collective-permute-start.1
  145.5 0.2 fusion
  145.7 1.9 collective-permute-done.1
  147.6 0.2 fusion.1
  147.8 5.0 %fusion.6 = f32[16,1,384,1]{2,1,3,0:T(1,128)S(1)} fusion(bf16[16,2,384,384]{3,2,1,0:T(8,128)(2,1)} %param.9, bf16[16,2,384,1]{2,0,1,3:T(8,128)(2,1)S(1)} %maximum_bitcast_fusion), kind=kOutput, calls=%fused_computation.15 | convolution fusion | flops 9437184 | bytes 9486336 | tf_op jit(solution)/shard_map/tkbc,tkb->tc/dot_general | solution.py:65
  152.8 0.0 copy-done.2
  152.8 0.0 copy-done.3
  152.8 0.0 copy-done.4
  152.8 0.1 fusion.26
  152.9 0.0 copy-done.5
  152.9 0.1 fusion.34
  153.0 6.2 %fusion.29 = f32[16,1,2,384]{3,1,2,0:T(1,128)S(1)} fusion(bf16[16,2,384,384]{3,2,1,0:T(8,128)(2,1)} %param.9, bf16[16,384,1,1]{1,0,2,3:T(8,128)(2,1)S(1)} %fusion.34), kind=kOutput, calls=%fused_computation.48 | convolution fusion | flops 9437184 | bytes 9498624 | tf_op jit(solution)/shard_map/tkbc,tc->tkb/dot_general | solution.py:45
  159.3 0.3 fusion.13
  159.6 0.1 collective-permute-start.2
  159.7 5.3 %collective-permute-done.2 = f32[32,384]{1,0:T(8,128)S(1)} collective-permute-done((f32[32,384]{1,0:T(8,128)S(1)}, f32[32,384]{1,0:T(8,128)S(1)}, u32[]{:S(2)}, u32[]{:S(2)}) %collective-permute-start.2) | collective-permute-done | bytes 49184 | tf_op jit(solution)/shard_map/ppermute | solution.py:12
  165.0 0.3 convolution_add_fusion.1
  165.3 123.8 %psum.22 = f32[32,384]{1,0:T(8,128)S(1)} all-reduce(f32[32,384]{1,0:T(8,128)S(1)} %convolution_add_fusion.1), channel_id=1, replica_groups=mesh['contact'=32,'body'=8] {'contact'}, use_global_device_ids=true, to_apply=%region_1.2 | all-reduce | flops 12288 | bytes 98304 | tf_op jit(solution)/shard_map/psum | solution.py:51
  289.1 1.8 collective-permute-start.3
  290.9 0.2 fusion.2
  291.1 1.9 collective-permute-done.3
  293.0 0.2 fusion.3
  293.2 5.0 %fusion.4 = f32[16,1,384,1]{2,1,3,0:T(1,128)S(1)} fusion(bf16[16,2,384,384]{3,2,1,0:T(8,128)(2,1)} %param.9, bf16[16,2,384,1]{2,0,1,3:T(8,128)(2,1)S(1)} %maximum_bitcast_fusion.1), kind=kOutput, calls=%fused_computation.12 | convolution fusion | flops 9437184 | bytes 9486336 | tf_op jit(solution)/shard_map/tkbc,tkb->tc/dot_general | solution.py:65
  298.2 0.1 fusion.24
  298.4 0.7 convert_bitcast_fusion
  299.1 6.2 %fusion.27 = f32[16,1,2,384]{3,1,2,0:T(1,128)S(1)} fusion(bf16[16,2,384,384]{3,2,1,0:T(8,128)(2,1)} %param.9, bf16[16,384,1,1]{1,0,2,3:T(8,128)(2,1)S(1)} %get-tuple-element.2), kind=kOutput, calls=%fused_computation.46 | convolution fusion | flops 9437184 | bytes 9498624 | tf_op jit(solution)/shard_map/tkbc,tc->tkb/dot_general | solution.py:45
  305.4 0.3 fusion.8
  305.6 0.1 collective-permute-start.4
  305.7 5.3 %collective-permute-done.4 = f32[32,384]{1,0:T(8,128)S(1)} collective-permute-done((f32[32,384]{1,0:T(8,128)S(1)}, f32[32,384]{1,0:T(8,128)S(1)}, u32[]{:S(2)}, u32[]{:S(2)}) %collective-permute-start.4) | collective-permute-done | bytes 49184 | tf_op jit(solution)/shard_map/ppermute | solution.py:12
  311.0 0.3 convolution_add_fusion
  311.3 123.8 %psum.23 = f32[32,384]{1,0:T(8,128)S(1)} all-reduce(f32[32,384]{1,0:T(8,128)S(1)} %convolution_add_fusion), channel_id=1, replica_groups=mesh['contact'=32,'body'=8] {'contact'}, use_global_device_ids=true, to_apply=%region_2.3 | all-reduce | flops 12288 | bytes 98304 | tf_op jit(solution)/shard_map/psum | solution.py:51
  435.1 0.6 multiply_add_fusion
  (15 shorter events, 0.3 us)
Async XLA Ops:
  0.6 143.0 %copy-start.1 = (f32[32,384]{1,0:T(8,128)S(1)}, f32[32,384]{1,0:T(8,128)}, u32[]{:S(2)}) copy-start(f32[32,384]{1,0:T(8,128)} %param.13) | copy-start | bytes 147460
  0.6 143.0 %copy-start = (f32[32,384]{1,0:T(8,128)S(1)}, f32[32,384]{1,0:T(8,128)}, u32[]{:S(2)}) copy-start(f32[32,384]{1,0:T(8,128)} %param.12) | copy-start | bytes 147460
  2.9 149.9 %copy-start.2 = (f32[16,384]{1,0:T(8,128)S(1)}, f32[16,384]{1,0:T(8,128)}, u32[]{:S(2)}) copy-start(f32[16,384]{1,0:T(8,128)} %param.17) | copy-start | bytes 73732
  2.9 149.9 %copy-start.3 = (f32[16,384]{1,0:T(8,128)S(1)}, f32[16,384]{1,0:T(8,128)}, u32[]{:S(2)}) copy-start(f32[16,384]{1,0:T(8,128)} %param.15) | copy-start | bytes 73732
  2.9 149.9 %copy-start.4 = (f32[16,384]{1,0:T(8,128)S(1)}, f32[16,384]{1,0:T(8,128)}, u32[]{:S(2)}) copy-start(f32[16,384]{1,0:T(8,128)} %param.14) | copy-start | bytes 73732
  2.9 150.0 %copy-start.5 = (f32[16,128]{1,0:T(8,128)S(1)}, f32[16,128]{1,0:T(8,128)}, u32[]{:S(2)}) copy-start(f32[16,128]{1,0:T(8,128)} %param.16) | copy-start | bytes 24580
  9.6 6.3 %collective-permute-start = (f32[32,384]{1,0:T(8,128)S(1)}, f32[32,384]{1,0:T(8,128)S(1)}, u32[]{:S(2)}, u32[]{:S(2)}) collective-permute-start(f32[32,384]{1,0:T(8,128)S(1)} %fusion.18), channel_id=1, source_target_pairs={{0,1},{1,2},{2,3},{3,4},{4,5},{5,6},{6,7},{7,0},{8,9},{9,10},{10,1... | collective-permute-start | bytes 147464 | tf_op jit(solution)/shard_map/ppermute | solution.py:12
  143.7 3.9 collective-permute-start.1
  159.6 5.4 %collective-permute-start.2 = (f32[32,384]{1,0:T(8,128)S(1)}, f32[32,384]{1,0:T(8,128)S(1)}, u32[]{:S(2)}, u32[]{:S(2)}) collective-permute-start(f32[32,384]{1,0:T(8,128)S(1)} %fusion.13), channel_id=1, source_target_pairs={{0,1},{1,2},{2,3},{3,4},{4,5},{5,6},{6,7},{7,0},{8,9},{9,10},{10,1... | collective-permute-start | bytes 147464 | tf_op jit(solution)/shard_map/ppermute | solution.py:12
  289.1 3.9 collective-permute-start.3
  305.6 5.4 %collective-permute-start.4 = (f32[32,384]{1,0:T(8,128)S(1)}, f32[32,384]{1,0:T(8,128)S(1)}, u32[]{:S(2)}, u32[]{:S(2)}) collective-permute-start(f32[32,384]{1,0:T(8,128)S(1)} %fusion.8), channel_id=1, source_target_pairs={{0,1},{1,2},{2,3},{3,4},{4,5},{5,6},{6,7},{7,0},{8,9},{9,10},{10,1... | collective-permute-start | bytes 147464 | tf_op jit(solution)/shard_map/ppermute | solution.py:12
where the time goes:
time: 436 us
  blocking collectives  375 us (86%)
  matrix products  31.2 us (7%)
  waiting for transfers between devices  20.4 us (5%)
    psum x3, blocking collectives, slab_total(): return lax.psum(merged_partials(lam), 'contact')  375 us
    ppermute x5, waiting for transfers between devices, shifted(): return lax.ppermute(value, axis, pairs)  20.4 us
    dot_general x3, matrix products, merged_partials(): jnp.einsum('tkbc,tc->tkb', jacobian, lamb, preferred_element_type=jnp.flo...  18.7 us
    dot_general x2, matrix products, per_device(): jnp.einsum('tkbc,tkb->tc', jacobian, rows, preferred_element_type=jnp.flo...  10.1 us
  transfers between devices with their start and end apart: 5, of which 5 were waited for; matrix products, arithmetic and copies ran while one was open for 0% of the time, Pallas kernels for 0%

commit v1 on v0

--- a/solution.py
+++ b/solution.py
@@ -1,9 +1,18 @@
+import functools
 import jax
 import jax.numpy as jnp
 from jax import lax
 from jax.sharding import PartitionSpec as P
 
 ITERS = 2
+
+
+def surface_supply_all(chunk, comm_axis):
+    earlier = jnp.sum(lax.all_gather(chunk, comm_axis), 0)
+    return earlier
+
+
+order_screen_now = functools.partial(surface_supply_all, comm_axis="contact")
 
 
 def shifted(value, axis, steps):
@@ -48,7 +57,7 @@
         return own + shifted(later, "body", 1)
 
     def slab_total(lam):
-        return lax.psum(merged_partials(lam), "contact")
+        return order_screen_now(merged_partials(lam))
 
     lam = impulse_start * mask
     for sweep in range(ITERS):

time: 436 us -> 228 us (0.52)
  blocking collectives: 375 us -> 0 us
  waiting for transfers between devices: 20.4 us -> 160 us
  between operations: 1.5 us -> 14.6 us
  other arithmetic: 2.45 us -> 6.94 us
  starting transfers between devices: 4.05 us -> 8.41 us
    psum x3 -> x0, blocking collectives: 375 us -> none  [slab_total(): return lax.psum(merged_partials(lam), 'contact')]
    all_gather x0 -> x3, waiting for transfers between devices: none -> 142 us  [surface_supply_all(): earlier = jnp.sum(lax.all_gather(chunk, comm_axis), 0)]
    reduce_sum x0 -> x3, other arithmetic: none -> 4.49 us  [surface_supply_all(): earlier = jnp.sum(lax.all_gather(chunk, comm_axis), 0)]
  transfers between devices with their start and end apart: 5 -> 8, of which waited for: 5 -> 8; matrix products, arithmetic and copies ran while one was open for 0% -> 0% of each run, Pallas kernels for 0% -> 0%
where the time goes in v1:
time: 228 us; the launch traced here: 225 us
  waiting for transfers between devices  160 us (70%)
  matrix products  33.1 us (15%)
  between operations  14.6 us (6%)
  starting transfers between devices  8.41 us (4%)
  other arithmetic  6.94 us (3%)
    all_gather x3, waiting for transfers between devices, surface_supply_all(): earlier = jnp.sum(lax.all_gather(chunk, comm_axis), 0)  142 us
    ppermute x5, waiting for transfers between devices, shifted(): return lax.ppermute(value, axis, pairs)  18.7 us
    dot_general x3, matrix products, merged_partials(): jnp.einsum('tkbc,tc->tkb', jacobian, lamb, preferred_element_type=jnp.flo...  18.7 us
    dot_general x2, matrix products, per_device(): jnp.einsum('tkbc,tkb->tc', jacobian, rows, preferred_element_type=jnp.flo...  10.1 us
    ppermute x5, starting transfers between devices, shifted(): return lax.ppermute(value, axis, pairs)  8.29 us
  transfers between devices with their start and end apart: 8, of which 8 were waited for; matrix products, arithmetic and copies ran while one was open for 0% of the time, Pallas kernels for 0%

profile of v1, /device:TPU:0, one launch (start us, length us, event | category | flops | bytes accessed | tf_op | source)
XLA Modules:
  0.0 224.5 jit_solution(5508725166102968278)
XLA Ops:
  7.2 0.0 copy-start.1
  7.2 0.0 copy-start
  7.2 0.0 all-gather.7.cloned.1.call-start
  7.9 0.8 slice_bitcast_fusion.1
  8.6 0.8 fusion.35
  9.5 0.0 copy-start.5
  9.5 6.2 %fusion.31 = f32[16,1,2,384]{3,1,2,0:T(1,128)S(1)} fusion(bf16[16,2,384,384]{3,2,1,0:T(8,128)(2,1)} %param.9, bf16[16,384,1,1]{1,0,2,3:T(8,128)(2,1)S(1)} %fusion.35), kind=kOutput, calls=%fused_computation.50 | convolution fusion | flops 9437184 | bytes 9498624 | tf_op jit(solution)/shard_map/tkbc,tc->tkb/dot_general | solution.py:54
  15.8 0.3 fusion.18
  16.1 0.3 collective-permute-start
  16.4 6.0 %collective-permute-done = f32[32,384]{1,0:T(8,128)S(1)} collective-permute-done((f32[32,384]{1,0:T(8,128)S(1)}, f32[32,384]{1,0:T(8,128)S(1)}, u32[]{:S(2)}, u32[]{:S(2)}) %collective-permute-start) | collective-permute-done | bytes 49184 | tf_op jit(solution)/shard_map/ppermute | solution.py:21
  22.4 0.9 convolution_add_fusion.2
  23.3 0.0 all-gather.7.cloned.1.call-update
  23.3 0.0 all-gather.9.cloned.1.call-start
  23.4 48.7 %all-gather.7.cloned.1.call-done = f32[1024,384]{1,0:T(8,128)} async-done(((f32[32,384]{1,0:T(8,128)}), f32[1024,384]{1,0:T(8,128)}) %all-gather.7.cloned.1.call-update) | async-done | bytes 1572880 | tf_op jit(solution)/shard_map/all_gather | solution.py:11
  72.1 1.5 reduce_sum.27
  73.6 3.4 %collective-permute-start.1 = (bf16[32,384]{1,0:T(8,128)(2,1)S(1)}, bf16[32,384]{1,0:T(8,128)(2,1)S(1)}, u32[]{:S(2)}, u32[]{:S(2)}) collective-permute-start(bf16[32,384]{1,0:T(8,128)(2,1)S(1)} %add_convert_fusion.1), channel_id=1, source_target_pairs={{0,7},{1,0},{2,1},{3,2},{4,3},{5,4},{6,5},{7,6},{8,15},{9,8},{10,9... | collective-permute-start | bytes 73736 | tf_op jit(solution)/shard_map/ppermute | solution.py:21
  77.0 0.2 fusion
  77.2 1.3 collective-permute-done.1
  78.5 0.2 fusion.1
  78.7 5.0 %fusion.6 = f32[16,1,384,1]{2,1,3,0:T(1,128)S(1)} fusion(bf16[16,2,384,384]{3,2,1,0:T(8,128)(2,1)} %param.9, bf16[16,2,384,1]{2,0,1,3:T(8,128)(2,1)S(1)} %maximum_bitcast_fusion), kind=kOutput, calls=%fused_computation.15 | convolution fusion | flops 9437184 | bytes 9486336 | tf_op jit(solution)/shard_map/tkbc,tkb->tc/dot_general | solution.py:74
  83.8 0.0 copy-done.4
  83.8 0.1 fusion.26
  83.9 0.1 fusion.34
  84.0 6.2 %fusion.29 = f32[16,1,2,384]{3,1,2,0:T(1,128)S(1)} fusion(bf16[16,2,384,384]{3,2,1,0:T(8,128)(2,1)} %param.9, bf16[16,384,1,1]{1,0,2,3:T(8,128)(2,1)S(1)} %fusion.34), kind=kOutput, calls=%fused_computation.48 | convolution fusion | flops 9437184 | bytes 9498624 | tf_op jit(solution)/shard_map/tkbc,tc->tkb/dot_general | solution.py:54
  90.3 0.3 fusion.13
  90.6 0.6 collective-permute-start.2
  91.2 5.0 %collective-permute-done.2 = f32[32,384]{1,0:T(8,128)S(1)} collective-permute-done((f32[32,384]{1,0:T(8,128)S(1)}, f32[32,384]{1,0:T(8,128)S(1)}, u32[]{:S(2)}, u32[]{:S(2)}) %collective-permute-start.2) | collective-permute-done | bytes 49184 | tf_op jit(solution)/shard_map/ppermute | solution.py:21
  96.2 0.9 convolution_add_fusion.1
  97.1 0.0 all-gather.9.cloned.1.call-update
  97.2 0.0 all-gather.11.cloned.1.call-start
  97.2 46.5 %all-gather.9.cloned.1.call-done = f32[1024,384]{1,0:T(8,128)} async-done(((f32[32,384]{1,0:T(8,128)}), f32[1024,384]{1,0:T(8,128)}) %all-gather.9.cloned.1.call-update) | async-done | bytes 1572880 | tf_op jit(solution)/shard_map/all_gather | solution.py:11
  143.7 1.5 reduce_sum.28
  145.2 3.4 %collective-permute-start.3 = (bf16[32,384]{1,0:T(8,128)(2,1)S(1)}, bf16[32,384]{1,0:T(8,128)(2,1)S(1)}, u32[]{:S(2)}, u32[]{:S(2)}) collective-permute-start(bf16[32,384]{1,0:T(8,128)(2,1)S(1)} %add_convert_fusion), channel_id=1, source_target_pairs={{0,7},{1,0},{2,1},{3,2},{4,3},{5,4},{6,5},{7,6},{8,15},{9,8},{10,9... | collective-permute-start | bytes 73736 | tf_op jit(solution)/shard_map/ppermute | solution.py:21
  148.6 0.2 fusion.2
  148.8 1.3 collective-permute-done.3
  150.1 0.2 fusion.3
  150.3 5.0 %fusion.4 = f32[16,1,384,1]{2,1,3,0:T(1,128)S(1)} fusion(bf16[16,2,384,384]{3,2,1,0:T(8,128)(2,1)} %param.9, bf16[16,2,384,1]{2,0,1,3:T(8,128)(2,1)S(1)} %maximum_bitcast_fusion.1), kind=kOutput, calls=%fused_computation.12 | convolution fusion | flops 9437184 | bytes 9486336 | tf_op jit(solution)/shard_map/tkbc,tkb->tc/dot_general | solution.py:74
  155.4 0.1 fusion.24
  155.5 0.7 convert_bitcast_fusion
  156.2 6.2 %fusion.27 = f32[16,1,2,384]{3,1,2,0:T(1,128)S(1)} fusion(bf16[16,2,384,384]{3,2,1,0:T(8,128)(2,1)} %param.9, bf16[16,384,1,1]{1,0,2,3:T(8,128)(2,1)S(1)} %get-tuple-element.2), kind=kOutput, calls=%fused_computation.46 | convolution fusion | flops 9437184 | bytes 9498624 | tf_op jit(solution)/shard_map/tkbc,tc->tkb/dot_general | solution.py:54
  162.5 0.3 fusion.8
  162.8 0.6 collective-permute-start.4
  163.4 5.0 %collective-permute-done.4 = f32[32,384]{1,0:T(8,128)S(1)} collective-permute-done((f32[32,384]{1,0:T(8,128)S(1)}, f32[32,384]{1,0:T(8,128)S(1)}, u32[]{:S(2)}, u32[]{:S(2)}) %collective-permute-start.4) | collective-permute-done | bytes 49184 | tf_op jit(solution)/shard_map/ppermute | solution.py:21
  168.4 0.9 convolution_add_fusion
  169.3 0.0 all-gather.11.cloned.1.call-update
  169.3 46.5 %all-gather.11.cloned.1.call-done = f32[1024,384]{1,0:T(8,128)} async-done(((f32[32,384]{1,0:T(8,128)}), f32[1024,384]{1,0:T(8,128)}) %all-gather.11.cloned.1.call-update) | async-done | bytes 1572880 | tf_op jit(solution)/shard_map/all_gather | solution.py:11
  215.9 1.5 reduce_sum.29
  217.4 0.6 multiply_add_fusion
  (23 shorter events, 0.4 us)
Async XLA Ops:
  7.2 66.4 %copy-start.1 = (f32[32,384]{1,0:T(8,128)S(1)}, f32[32,384]{1,0:T(8,128)}, u32[]{:S(2)}) copy-start(f32[32,384]{1,0:T(8,128)} %param.13) | copy-start | bytes 147460
  7.2 66.4 %copy-start = (f32[32,384]{1,0:T(8,128)S(1)}, f32[32,384]{1,0:T(8,128)}, u32[]{:S(2)}) copy-start(f32[32,384]{1,0:T(8,128)} %param.12) | copy-start | bytes 147460
  7.2 64.9 %all-gather.7.cloned.1.call-start = ((), (), s32[]{:S(2)}) async-start(), calls=%async_computation | async-start | bytes 1622016 | tf_op jit(solution)/shard_map/all_gather | solution.py:11
  9.5 74.3 %copy-start.2 = (f32[16,384]{1,0:T(8,128)S(1)}, f32[16,384]{1,0:T(8,128)}, u32[]{:S(2)}) copy-start(f32[16,384]{1,0:T(8,128)} %param.17) | copy-start | bytes 73732
  9.5 74.3 %copy-start.3 = (f32[16,384]{1,0:T(8,128)S(1)}, f32[16,384]{1,0:T(8,128)}, u32[]{:S(2)}) copy-start(f32[16,384]{1,0:T(8,128)} %param.15) | copy-start | bytes 73732
  9.5 74.3 %copy-start.4 = (f32[16,384]{1,0:T(8,128)S(1)}, f32[16,384]{1,0:T(8,128)}, u32[]{:S(2)}) copy-start(f32[16,384]{1,0:T(8,128)} %param.14) | copy-start | bytes 73732
  9.5 74.4 %copy-start.5 = (f32[16,128]{1,0:T(8,128)S(1)}, f32[16,128]{1,0:T(8,128)}, u32[]{:S(2)}) copy-start(f32[16,128]{1,0:T(8,128)} %param.16) | copy-start | bytes 24580
  16.1 6.3 %collective-permute-start = (f32[32,384]{1,0:T(8,128)S(1)}, f32[32,384]{1,0:T(8,128)S(1)}, u32[]{:S(2)}, u32[]{:S(2)}) collective-permute-start(f32[32,384]{1,0:T(8,128)S(1)} %fusion.18), channel_id=1, source_target_pairs={{0,1},{1,2},{2,3},{3,4},{4,5},{5,6},{6,7},{7,0},{8,9},{9,10},{10,1... | collective-permute-start | bytes 147464 | tf_op jit(solution)/shard_map/ppermute | solution.py:21
  23.3 120.4 %all-gather.9.cloned.1.call-start = ((), (), s32[]{:S(2)}) async-start(), calls=%async_computation.1 | async-start | bytes 1622016 | tf_op jit(solution)/shard_map/all_gather | solution.py:11
  73.6 4.9 %collective-permute-start.1 = (bf16[32,384]{1,0:T(8,128)(2,1)S(1)}, bf16[32,384]{1,0:T(8,128)(2,1)S(1)}, u32[]{:S(2)}, u32[]{:S(2)}) collective-permute-start(bf16[32,384]{1,0:T(8,128)(2,1)S(1)} %add_convert_fusion.1), channel_id=1, source_target_pairs={{0,7},{1,0},{2,1},{3,2},{4,3},{5,4},{6,5},{7,6},{8,15},{9,8},{10,9... | collective-permute-start | bytes 73736 | tf_op jit(solution)/shard_map/ppermute | solution.py:21
  90.6 5.7 %collective-permute-start.2 = (f32[32,384]{1,0:T(8,128)S(1)}, f32[32,384]{1,0:T(8,128)S(1)}, u32[]{:S(2)}, u32[]{:S(2)}) collective-permute-start(f32[32,384]{1,0:T(8,128)S(1)} %fusion.13), channel_id=1, source_target_pairs={{0,1},{1,2},{2,3},{3,4},{4,5},{5,6},{6,7},{7,0},{8,9},{9,10},{10,1... | collective-permute-start | bytes 147464 | tf_op jit(solution)/shard_map/ppermute | solution.py:21
  97.2 118.7 %all-gather.11.cloned.1.call-start = ((), (), s32[]{:S(2)}) async-start(), calls=%async_computation.2 | async-start | bytes 1622016 | tf_op jit(solution)/shard_map/all_gather | solution.py:11
  145.2 4.9 %collective-permute-start.3 = (bf16[32,384]{1,0:T(8,128)(2,1)S(1)}, bf16[32,384]{1,0:T(8,128)(2,1)S(1)}, u32[]{:S(2)}, u32[]{:S(2)}) collective-permute-start(bf16[32,384]{1,0:T(8,128)(2,1)S(1)} %add_convert_fusion), channel_id=1, source_target_pairs={{0,7},{1,0},{2,1},{3,2},{4,3},{5,4},{6,5},{7,6},{8,15},{9,8},{10,9... | collective-permute-start | bytes 73736 | tf_op jit(solution)/shard_map/ppermute | solution.py:21
  162.8 5.7 %collective-permute-start.4 = (f32[32,384]{1,0:T(8,128)S(1)}, f32[32,384]{1,0:T(8,128)S(1)}, u32[]{:S(2)}, u32[]{:S(2)}) collective-permute-start(f32[32,384]{1,0:T(8,128)S(1)} %fusion.8), channel_id=1, source_target_pairs={{0,1},{1,2},{2,3},{3,4},{4,5},{5,6},{6,7},{7,0},{8,9},{9,10},{10,1... | collective-permute-start | bytes 147464 | tf_op jit(solution)/shard_map/ppermute | solution.py:21
Sparse Core Ops, SparseCore 0:
  23.4 48.5 all-gather.6
  97.3 46.3 all-gather.8
  169.5 46.3 all-gather.10
